TPU v7x, 256 devices: a whole 4x4x8 slice. The times are simulated.
256 devices in a mesh: gx: 32 (over x, z_hi, core), sec: 8 (over z_lo, y).
Axes of the slice: x: 4, y: 4, z: 8 (z_hi: 4, z_lo: 2; z = z_hi * 2 + z_lo), core: 2. Of those that a mesh axis runs over, the one named last changes fastest.
Arguments:
- state_init: float32 [16, 256, 64, 128], P(None, 'gx', 'sec'), may hold values from -6 to 6
- rock_type: int32 [256, 4096], P('gx', 'sec'), may hold values from 0 to 15
- perm_table: float32 [3, 16], replicated, may hold values from 0.2 to 1
- well_cells: int32 [256], replicated, may hold values from 0 to 1048575
- well_rate: float32 [16, 256], replicated, may hold values from -12 to 12
- basis_in: bfloat16 [256, 64, 128, 256], P(('gx', 'sec')), may hold values from -4 to 4
- singular: float32 [256], replicated, may hold values from 0.5 to 2
Outputs:
- state_out: float32 [16, 256, 64, 128], P(None, 'gx', 'sec')
- basis_out: bfloat16 [256, 64, 128, 256], P(('gx', 'sec'))
- singular_out: float32 [256], replicated
All inputs are finite; a program needn't handle non-finite values.
Results may differ from a plain program's by a relative error of at most 0.0059.
Values may be sent and summed in bfloat16 or wider, within the bound.
A program may use at most 128 MiB of HBM per device.

v0:
```python
import jax
import jax.numpy as jnp
from jax import lax
from jax.sharding import PartitionSpec as P

MG = 8
STEPS = 4
GROUPS = 2
DT_PRESSURE = 0.12
DT_SATURATION = 0.06
DT_ADVECT = 0.15


def with_halo(block, sides, width):
    for axis, dim in sides:
        count = lax.axis_size(axis)
        forward = [(i, i + 1) for i in range(count - 1)]
        backward = [(target, source) for source, target in forward]
        low = lax.ppermute(
            lax.slice_in_dim(block, block.shape[dim] - width, None, axis=dim), axis, forward
        )
        high = lax.ppermute(lax.slice_in_dim(block, 0, width, axis=dim), axis, backward)
        block = jnp.concatenate([low, block, high], axis=dim)
    return block


def harmonic(left, right):
    return 2.0 * left * right / (left + right)


def shift_layers(fields):
    blank = jnp.zeros_like(fields[..., :1])
    return (
        jnp.concatenate([fields[..., 1:], blank], -1),
        jnp.concatenate([blank, fields[..., :-1]], -1),
    )


def advance(fields, besides, weights, inflow, layers):
    column = lax.broadcasted_iota(jnp.int32, (fields.shape[-1],), 0)
    step_sizes = jnp.where(column < layers, DT_PRESSURE, DT_SATURATION)
    is_sat = (column >= layers).astype(fields.dtype)
    press_both = jnp.concatenate([fields[..., :layers], fields[..., :layers]], -1)
    spread = jnp.zeros_like(fields)
    carried = jnp.zeros_like(fields)
    for beside, weight in zip(besides, weights):
        spread = spread + weight * (beside - fields)
        beside_press = jnp.concatenate([beside[..., :layers], beside[..., :layers]], -1)
        pushed = weight * (beside_press - press_both)
        carried = carried + jnp.maximum(pushed, 0.0) * beside + jnp.minimum(pushed, 0.0) * fields
    return fields + step_sizes * spread + DT_ADVECT * is_sat * carried + DT_PRESSURE * inflow


def small_rotation(coeffs, lower, sigma):
    count = sigma.shape[0]
    extra = lower.shape[0]
    top = jnp.concatenate([jnp.diag(sigma), coeffs.T], 1)
    bottom = jnp.concatenate([jnp.zeros((extra, count), sigma.dtype), lower.T], 1)
    core = jnp.concatenate([top, bottom], 0)
    leading = jnp.dot(core, top.T, precision=lax.Precision.HIGHEST)
    inner = jnp.dot(leading.T, leading, precision=lax.Precision.HIGHEST)
    factor = jnp.linalg.cholesky(inner)
    rotation = lax.linalg.triangular_solve(factor, leading.T, left_side=True, lower=True).T
    energy = jnp.dot(core.T, rotation, precision=lax.Precision.HIGHEST)
    return (rotation, jnp.sqrt(jnp.sum(energy * energy, axis=0)))


def compress(stacked, basis_now, sigma, rows_total):
    count = stacked.shape[0]
    snaps = stacked.reshape(count, -1)
    flat_basis = basis_now.reshape(snaps.shape[1], basis_now.shape[-1])
    basis_count = flat_basis.shape[1]
    local_proj = jnp.dot(snaps, flat_basis, preferred_element_type=jnp.float32)
    coeffs = lax.psum(local_proj, ("gx", "sec")) / rows_total
    rounded = coeffs.astype(jnp.bfloat16)
    resid = snaps.astype(jnp.float32) - lax.dot_general(
        rounded, flat_basis, (((1,), (1,)), ((), ())), preferred_element_type=jnp.float32
    )
    gram = (
        lax.psum(jnp.dot(resid, resid.T, precision=lax.Precision.HIGHEST), ("gx", "sec"))
        / rows_total
    )
    lower = jnp.linalg.cholesky(gram)
    ortho = lax.linalg.triangular_solve(lower, resid, left_side=True, lower=True).astype(
        jnp.bfloat16
    )
    rotation, sigma_next = small_rotation(coeffs, lower, sigma)
    mixing = rotation.astype(jnp.bfloat16)
    fresh = jnp.dot(flat_basis, mixing[:basis_count], preferred_element_type=jnp.float32)
    fresh = fresh + lax.dot_general(
        ortho, mixing[basis_count:], (((0,), (0,)), ((), ())), preferred_element_type=jnp.float32
    )
    return (fresh.astype(jnp.bfloat16).reshape(basis_now.shape), sigma_next)


def body(state_init, rock_type, perm_table, well_cells, well_rate, basis_in, singular):
    across = state_init.shape[1]
    along = state_init.shape[2]
    layers = state_init.shape[3] // 2
    sec_count = lax.axis_size("sec")
    rock_count = perm_table.shape[1]
    kinds = lax.broadcasted_iota(jnp.int32, (rock_count, 1, 1), 0)
    picks = (rock_type[None] == kinds).astype(jnp.float32)
    perm = jnp.einsum("dr,rxc->dxc", perm_table, picks, precision=lax.Precision.HIGHEST).reshape(
        3, across, along, layers
    )
    paired = jnp.concatenate([perm[0], perm[1]], -1)
    bordered_perm = with_halo(paired.astype(jnp.bfloat16), (("gx", 0), ("sec", 1)), 1).astype(
        paired.dtype
    )
    perm_xh = bordered_perm[..., :layers]
    perm_yh = bordered_perm[..., layers:]
    x_up = harmonic(perm[0], perm_xh[2:, 1:-1])
    x_down = harmonic(perm_xh[:-2, 1:-1], perm[0])
    y_up = harmonic(perm[1], perm_yh[1:-1, 2:])
    y_down = harmonic(perm_yh[1:-1, :-2], perm[1])
    z_padded = jnp.pad(perm[2], ((0, 0), (0, 0), (1, 1)))
    z_up = harmonic(perm[2], z_padded[..., 2:])
    z_down = harmonic(z_padded[..., :-2], perm[2])
    weights = [
        jnp.concatenate([face, face], -1) for face in (x_up, x_down, y_up, y_down, z_up, z_down)
    ]
    x_start = lax.axis_index("gx") * across
    y_start = lax.axis_index("sec") * along
    total_y = along * sec_count
    x_pos = lax.broadcasted_iota(jnp.int32, (across, along, layers), 0)
    y_pos = lax.broadcasted_iota(jnp.int32, (across, along, layers), 1)
    z_pos = lax.broadcasted_iota(jnp.int32, (across, along, layers), 2)
    cell_ids = ((x_start + x_pos) * total_y + y_start + y_pos) * layers + z_pos
    hits = (well_cells[:, None] == cell_ids.reshape(1, -1)).astype(jnp.float32)
    source = jnp.dot(well_rate, hits, precision=lax.Precision.HIGHEST).reshape(
        state_init.shape[0], across, along, layers
    )
    source_full = jnp.concatenate([source, jnp.zeros_like(source)], -1)
    local_rows = basis_in.shape[0] * basis_in.shape[1] * basis_in.shape[2]
    rows_total = local_rows * lax.axis_size("gx") * sec_count
    basis_now = basis_in
    sigma = singular
    finals = []
    for group in range(GROUPS):
        fields = state_init[group * MG : (group + 1) * MG]
        inflow = source_full[group * MG : (group + 1) * MG]
        saved = []
        for step_index in range(STEPS):
            bordered = with_halo(fields.astype(jnp.bfloat16), (("gx", 1), ("sec", 2)), 1).astype(
                fields.dtype
            )
            up_layer, down_layer = shift_layers(fields)
            besides = [
                bordered[:, 2:, 1:-1],
                bordered[:, :-2, 1:-1],
                bordered[:, 1:-1, 2:],
                bordered[:, 1:-1, :-2],
                up_layer,
                down_layer,
            ]
            fields = advance(fields, besides, weights, inflow, layers)
            snapshot = fields.astype(jnp.bfloat16)
            saved.append(snapshot)
        finals.append(fields)
        stacked = jnp.concatenate(saved, 0)
        stacked = lax.all_to_all(stacked, "sec", split_axis=1, concat_axis=2, tiled=True)
        basis_now, sigma = compress(stacked, basis_now, sigma, rows_total)
    return (jnp.concatenate(finals, 0), basis_now, sigma)


def solution(mesh):
    return jax.shard_map(
        body,
        mesh=mesh,
        in_specs=(
            P(None, "gx", "sec", None),
            P("gx", "sec"),
            P(),
            P(),
            P(),
            P(("gx", "sec"), None, None, None),
            P(),
        ),
        out_specs=(P(None, "gx", "sec", None), P(("gx", "sec"), None, None, None), P()),
        check_vma=False,
    )
```

profile of v0, /device:TPU:1, one launch (start us, length us, event | category | flops | bytes accessed | tf_op | source)
XLA Modules:
  0.0 677.7 jit_solution(60793899374076487)
XLA Ops:
  2.6 6.3 collective-permute-start
  61.2 7.0 %collective-permute-start.8 = (bf16[8,1,8,128]{3,2,0,1:T(8,128)(2,1)S(1)}, bf16[8,1,8,128]{3,2,0,1:T(8,128)(2,1)S(1)}, u32[]{:S(2)}, u32[]{:S(2)}) collective-permute-start(bf16[8,1,8,128]{3,2,0,1:T(8,128)(2,1)S(1)} %get-tuple-element.151), channel_id=1, source_target_pairs={{0,8},{8,16},{16,24},{24,32},{32,40},{40,48},{48,56},{56,64},{64,7... | collective-permute-start | bytes 49160 | tf_op jit(solution)/shard_map/ppermute | solution.py:19
  70.3 4.5 collective-permute-start.24
  82.6 5.3 collective-permute-start.26
  96.6 7.8 %collective-permute-start.12 = (bf16[8,1,8,128]{3,2,0,1:T(8,128)(2,1)S(1)}, bf16[8,1,8,128]{3,2,0,1:T(8,128)(2,1)S(1)}, u32[]{:S(2)}, u32[]{:S(2)}) collective-permute-start(bf16[8,1,8,128]{3,2,0,1:T(8,128)(2,1)S(1)} %get-tuple-element.149), channel_id=1, source_target_pairs={{0,8},{8,16},{16,24},{24,32},{32,40},{40,48},{48,56},{56,64},{64,7... | collective-permute-start | bytes 49160 | tf_op jit(solution)/shard_map/ppermute | solution.py:19
  106.6 4.5 collective-permute-start.28
  132.8 8.4 %collective-permute-start.16 = (bf16[8,1,8,128]{3,2,0,1:T(8,128)(2,1)S(1)}, bf16[8,1,8,128]{3,2,0,1:T(8,128)(2,1)S(1)}, u32[]{:S(2)}, u32[]{:S(2)}) collective-permute-start(bf16[8,1,8,128]{3,2,0,1:T(8,128)(2,1)S(1)} %get-tuple-element.147), channel_id=1, source_target_pairs={{0,8},{8,16},{16,24},{24,32},{32,40},{40,48},{48,56},{56,64},{64,7... | collective-permute-start | bytes 49160 | tf_op jit(solution)/shard_map/ppermute | solution.py:19
  143.3 4.5 collective-permute-start.32
  164.2 9.1 %all-to-all-start = ((bf16[32,8,8,128]{3,2,0,1:T(8,128)(2,1)}), bf16[32,8,8,128]{3,2,0,1:T(8,128)(2,1)S(1)}, u32[]{:S(2)}, u32[]{:S(2)}) async-start(bf16[32,8,8,128]{3,2,0,1:T(8,128)(2,1)} %pad_maximum_fusion.1), calls=%async_computation | async-start | bytes 1048576 | tf_op jit(solution)/shard_map/all_to_all | solution.py:162
  176.5 5.4 all-to-all-done
  188.5 89.6 %psum.28 = f32[32,256]{1,0:T(8,128)S(1)} all-reduce(f32[32,256]{1,0:T(8,128)S(1)} %fusion.9), channel_id=1, replica_groups=mesh['gx'=32,'sec'=8] {'gx','sec'}, use_global_device_ids=true, to_apply=%region_0.1 | all-reduce | flops 8192 | bytes 65536 | tf_op jit(solution)/shard_map/psum | solution.py:74
  282.7 74.5 %psum.29 = f32[32,32]{0,1:T(8,128)S(1)} all-reduce(f32[32,32]{0,1:T(8,128)S(1)} %fusion.171), channel_id=1, replica_groups=mesh['gx'=32,'sec'=8] {'gx','sec'}, use_global_device_ids=true, to_apply=%region_1.2 | all-reduce | flops 1024 | bytes 8192 | tf_op jit(solution)/shard_map/psum | solution.py:80
  363.2 11.7 %cholesky.183 = f32[128,128]{1,0:T(8,128)S(1)} custom-call(f32[128,128]{1,0:T(8,128)S(1)} %cholesky.258), custom_call_target="Cholesky" | custom-call | tf_op jit(solution)/shard_map/jit(cholesky)/cholesky | solution.py:62
  375.6 9.8 %custom-call.19 = f32[1,128,128]{1,2,0:T(8,128)S(1)} custom-call(f32[1,128,128]{2,1,0:T(8,128)S(1)} %get-tuple-element.176), custom_call_target="InvertDiagBlocksLowerTriangular" | custom-call | tf_op jit(solution)/shard_map/jit(cholesky)/cholesky | solution.py:62
  385.9 11.7 %cholesky.200 = f32[128,128]{1,0:T(8,128)S(1)} custom-call(f32[128,128]{1,0:T(8,128)S(1)} %convolution_subtract_fusion.5), custom_call_target="Cholesky" | custom-call | tf_op jit(solution)/shard_map/jit(cholesky)/cholesky | solution.py:62
  403.9 19.7 %custom-call.20 = f32[2,128,128]{1,2,0:T(8,128)S(1)} custom-call(f32[2,128,128]{2,1,0:T(8,128)S(1)} %get-tuple-element.21), custom_call_target="InvertDiagBlocksLowerTriangular" | custom-call | tf_op jit(solution)/shard_map/triangular_solve/custom-call.4 | solution.py:63
  424.5 6.8 %convolution_bitcast_fusion = f32[8192,256]{0,1:T(8,128)} fusion(bf16[8192,256]{1,0:T(8,128)(2,1)} %bitcast.138, bf16[288,256]{1,0:T(8,128)(2,1)S(1)} %fusion.85), kind=kOutput, calls=%fused_computation.6 | convolution fusion | flops 1073741824 | bytes 12713984 | tf_op jit(solution)/shard_map/dot_general | solution.py:89
  435.7 6.7 fusion
  446.1 73.6 %psum.30 = f32[32,256]{1,0:T(8,128)S(1)} all-reduce(f32[32,256]{1,0:T(8,128)S(1)} %fusion.7), channel_id=1, replica_groups=mesh['gx'=32,'sec'=8] {'gx','sec'}, use_global_device_ids=true, to_apply=%region_9.14 | all-reduce | flops 8192 | bytes 65536 | tf_op jit(solution)/shard_map/psum | solution.py:74
  524.0 74.3 %psum.31 = f32[32,32]{0,1:T(8,128)S(1)} all-reduce(f32[32,32]{0,1:T(8,128)S(1)} %fusion.173), channel_id=1, replica_groups=mesh['gx'=32,'sec'=8] {'gx','sec'}, use_global_device_ids=true, to_apply=%region_10.15 | all-reduce | flops 1024 | bytes 8192 | tf_op jit(solution)/shard_map/psum | solution.py:80
  604.4 11.7 %cholesky.228 = f32[128,128]{1,0:T(8,128)S(1)} custom-call(f32[128,128]{1,0:T(8,128)S(1)} %cholesky.261), custom_call_target="Cholesky" | custom-call | tf_op jit(solution)/shard_map/jit(cholesky)/cholesky | solution.py:62
  616.8 9.8 %custom-call.22 = f32[1,128,128]{1,2,0:T(8,128)S(1)} custom-call(f32[1,128,128]{2,1,0:T(8,128)S(1)} %get-tuple-element.172), custom_call_target="InvertDiagBlocksLowerTriangular" | custom-call | tf_op jit(solution)/shard_map/jit(cholesky)/cholesky | solution.py:62
  627.1 11.7 %cholesky.245 = f32[128,128]{1,0:T(8,128)S(1)} custom-call(f32[128,128]{1,0:T(8,128)S(1)} %convolution_subtract_fusion.4), custom_call_target="Cholesky" | custom-call | tf_op jit(solution)/shard_map/jit(cholesky)/cholesky | solution.py:62
  644.8 19.7 %custom-call.23 = f32[2,128,128]{1,2,0:T(8,128)S(1)} custom-call(f32[2,128,128]{2,1,0:T(8,128)S(1)} %get-tuple-element.22), custom_call_target="InvertDiagBlocksLowerTriangular" | custom-call | tf_op jit(solution)/shard_map/triangular_solve/custom-call.4 | solution.py:63
  (282 shorter events, 186.0 us)
Async XLA Ops:
  2.6 29.3 %collective-permute-start = (bf16[1,8,128]{2,1,0:T(8,128)(2,1)}, bf16[1,8,128]{2,1,0:T(8,128)(2,1)}, u32[]{:S(2)}, u32[]{:S(2)}) collective-permute-start(bf16[1,8,128]{2,1,0:T(8,128)(2,1)} %get-tuple-element.179), channel_id=1, source_target_pairs={{0,8},{8,16},{16,24},{24,32},{32,40},{40,48},{48,56},{56,64},{64,7... | collective-permute-start | bytes 6152 | tf_op jit(solution)/shard_map/ppermute | solution.py:19
  8.9 23.1 %collective-permute-start.1 = (bf16[1,8,128]{2,1,0:T(8,128)(2,1)}, bf16[1,8,128]{2,1,0:T(8,128)(2,1)}, u32[]{:S(2)}, u32[]{:S(2)}) collective-permute-start(bf16[1,8,128]{2,1,0:T(8,128)(2,1)} %get-tuple-element.180), channel_id=1, source_target_pairs={{8,0},{16,8},{24,16},{32,24},{40,32},{48,40},{56,48},{64,56},{72,6... | collective-permute-start | bytes 6152 | tf_op jit(solution)/shard_map/ppermute | solution.py:22
  12.5 29.9 %collective-permute-start.4 = (bf16[8,1,8,128]{3,2,0,1:T(8,128)(2,1)}, bf16[8,1,8,128]{3,2,0,1:T(8,128)(2,1)}, u32[]{:S(2)}, u32[]{:S(2)}) collective-permute-start(bf16[8,1,8,128]{3,2,0,1:T(8,128)(2,1)} %get-tuple-element.153), channel_id=1, source_target_pairs={{0,8},{8,16},{16,24},{24,32},{32,40},{40,48},{48,56},{56,64},{64,7... | collective-permute-start | bytes 49160 | tf_op jit(solution)/shard_map/ppermute | solution.py:19
  17.0 25.4 %collective-permute-start.5 = (bf16[8,1,8,128]{3,2,0,1:T(8,128)(2,1)}, bf16[8,1,8,128]{3,2,0,1:T(8,128)(2,1)}, u32[]{:S(2)}, u32[]{:S(2)}) collective-permute-start(bf16[8,1,8,128]{3,2,0,1:T(8,128)(2,1)} %get-tuple-element.154), channel_id=1, source_target_pairs={{8,0},{16,8},{24,16},{32,24},{40,32},{48,40},{56,48},{64,56},{72,6... | collective-permute-start | bytes 49160 | tf_op jit(solution)/shard_map/ppermute | solution.py:22
  19.6 28.9 %collective-permute-start.20 = (bf16[8,1,8,128]{3,2,0,1:T(8,128)(2,1)}, bf16[8,1,8,128]{3,2,0,1:T(8,128)(2,1)}, u32[]{:S(2)}, u32[]{:S(2)}) collective-permute-start(bf16[8,1,8,128]{3,2,0,1:T(8,128)(2,1)} %get-tuple-element.161), channel_id=1, source_target_pairs={{0,8},{8,16},{16,24},{24,32},{32,40},{40,48},{48,56},{56,64},{64,7... | collective-permute-start | bytes 49160 | tf_op jit(solution)/shard_map/ppermute | solution.py:19
  39.3 9.2 %collective-permute-start.21 = (bf16[8,1,8,128]{3,2,0,1:T(8,128)(2,1)}, bf16[8,1,8,128]{3,2,0,1:T(8,128)(2,1)S(1)}, u32[]{:S(2)}, u32[]{:S(2)}) collective-permute-start(bf16[8,1,8,128]{3,2,0,1:T(8,128)(2,1)} %get-tuple-element.162), channel_id=1, source_target_pairs={{8,0},{16,8},{24,16},{32,24},{40,32},{48,40},{56,48},{64,56},{72,6... | collective-permute-start | bytes 49160 | tf_op jit(solution)/shard_map/ppermute | solution.py:22
  43.3 11.4 %collective-permute-start.6 = (bf16[8,10,1,128]{3,2,0,1:T(2,128)(2,1)S(1)}, bf16[8,10,1,128]{3,2,0,1:T(2,128)(2,1)S(1)}, u32[]{:S(2)}, u32[]{:S(2)}) collective-permute-start(bf16[8,10,1,128]{3,2,0,1:T(2,128)(2,1)S(1)} %get-tuple-element.137), channel_id=1, source_target_pairs={{0,1},{1,2},{2,3},{3,4},{4,5},{5,6},{6,7},{8,9},{9,10},{10,11},{11... | collective-permute-start | bytes 61448 | tf_op jit(solution)/shard_map/ppermute | solution.py:19
  61.2 15.7 %collective-permute-start.8 = (bf16[8,1,8,128]{3,2,0,1:T(8,128)(2,1)S(1)}, bf16[8,1,8,128]{3,2,0,1:T(8,128)(2,1)S(1)}, u32[]{:S(2)}, u32[]{:S(2)}) collective-permute-start(bf16[8,1,8,128]{3,2,0,1:T(8,128)(2,1)S(1)} %get-tuple-element.151), channel_id=1, source_target_pairs={{0,8},{8,16},{16,24},{24,32},{32,40},{40,48},{48,56},{56,64},{64,7... | collective-permute-start | bytes 49160 | tf_op jit(solution)/shard_map/ppermute | solution.py:19
  68.3 8.7 %collective-permute-start.9 = (bf16[8,1,8,128]{3,2,0,1:T(8,128)(2,1)S(1)}, bf16[8,1,8,128]{3,2,0,1:T(8,128)(2,1)S(1)}, u32[]{:S(2)}, u32[]{:S(2)}) collective-permute-start(bf16[8,1,8,128]{3,2,0,1:T(8,128)(2,1)S(1)} %get-tuple-element.152), channel_id=1, source_target_pairs={{8,0},{16,8},{24,16},{32,24},{40,32},{48,40},{56,48},{64,56},{72,6... | collective-permute-start | bytes 49160 | tf_op jit(solution)/shard_map/ppermute | solution.py:22
  70.3 11.6 %collective-permute-start.24 = (bf16[8,1,8,128]{3,2,0,1:T(8,128)(2,1)S(1)}, bf16[8,1,8,128]{3,2,0,1:T(8,128)(2,1)S(1)}, u32[]{:S(2)}, u32[]{:S(2)}) collective-permute-start(bf16[8,1,8,128]{3,2,0,1:T(8,128)(2,1)S(1)} %get-tuple-element.159), channel_id=1, source_target_pairs={{0,8},{8,16},{16,24},{24,32},{32,40},{40,48},{48,56},{56,64},{64,7... | collective-permute-start | bytes 49160 | tf_op jit(solution)/shard_map/ppermute | solution.py:19
  77.0 12.1 %collective-permute-start.10 = (bf16[8,10,1,128]{3,2,0,1:T(2,128)(2,1)S(1)}, bf16[8,10,1,128]{3,2,0,1:T(2,128)(2,1)S(1)}, u32[]{:S(2)}, u32[]{:S(2)}) collective-permute-start(bf16[8,10,1,128]{3,2,0,1:T(2,128)(2,1)S(1)} %get-tuple-element.135), channel_id=1, source_target_pairs={{0,1},{1,2},{2,3},{3,4},{4,5},{5,6},{6,7},{8,9},{9,10},{10,11},{11... | collective-permute-start | bytes 61448 | tf_op jit(solution)/shard_map/ppermute | solution.py:19
  96.6 16.5 %collective-permute-start.12 = (bf16[8,1,8,128]{3,2,0,1:T(8,128)(2,1)S(1)}, bf16[8,1,8,128]{3,2,0,1:T(8,128)(2,1)S(1)}, u32[]{:S(2)}, u32[]{:S(2)}) collective-permute-start(bf16[8,1,8,128]{3,2,0,1:T(8,128)(2,1)S(1)} %get-tuple-element.149), channel_id=1, source_target_pairs={{0,8},{8,16},{16,24},{24,32},{32,40},{40,48},{48,56},{56,64},{64,7... | collective-permute-start | bytes 49160 | tf_op jit(solution)/shard_map/ppermute | solution.py:19
  104.5 8.7 %collective-permute-start.13 = (bf16[8,1,8,128]{3,2,0,1:T(8,128)(2,1)S(1)}, bf16[8,1,8,128]{3,2,0,1:T(8,128)(2,1)S(1)}, u32[]{:S(2)}, u32[]{:S(2)}) collective-permute-start(bf16[8,1,8,128]{3,2,0,1:T(8,128)(2,1)S(1)} %get-tuple-element.150), channel_id=1, source_target_pairs={{8,0},{16,8},{24,16},{32,24},{40,32},{48,40},{56,48},{64,56},{72,6... | collective-permute-start | bytes 49160 | tf_op jit(solution)/shard_map/ppermute | solution.py:22
  106.6 11.6 %collective-permute-start.28 = (bf16[8,1,8,128]{3,2,0,1:T(8,128)(2,1)S(1)}, bf16[8,1,8,128]{3,2,0,1:T(8,128)(2,1)S(1)}, u32[]{:S(2)}, u32[]{:S(2)}) collective-permute-start(bf16[8,1,8,128]{3,2,0,1:T(8,128)(2,1)S(1)} %get-tuple-element.157), channel_id=1, source_target_pairs={{0,8},{8,16},{16,24},{24,32},{32,40},{40,48},{48,56},{56,64},{64,7... | collective-permute-start | bytes 49160 | tf_op jit(solution)/shard_map/ppermute | solution.py:19
  113.3 12.3 %collective-permute-start.14 = (bf16[8,10,1,128]{3,2,0,1:T(2,128)(2,1)S(1)}, bf16[8,10,1,128]{3,2,0,1:T(2,128)(2,1)S(1)}, u32[]{:S(2)}, u32[]{:S(2)}) collective-permute-start(bf16[8,10,1,128]{3,2,0,1:T(2,128)(2,1)S(1)} %get-tuple-element.133), channel_id=1, source_target_pairs={{0,1},{1,2},{2,3},{3,4},{4,5},{5,6},{6,7},{8,9},{9,10},{10,11},{11... | collective-permute-start | bytes 61448 | tf_op jit(solution)/shard_map/ppermute | solution.py:19
  116.9 8.7 %collective-permute-start.15 = (bf16[8,10,1,128]{3,2,0,1:T(2,128)(2,1)S(1)}, bf16[8,10,1,128]{3,2,0,1:T(2,128)(2,1)S(1)}, u32[]{:S(2)}, u32[]{:S(2)}) collective-permute-start(bf16[8,10,1,128]{3,2,0,1:T(2,128)(2,1)S(1)} %get-tuple-element.134), channel_id=1, source_target_pairs={{1,0},{2,1},{3,2},{4,3},{5,4},{6,5},{7,6},{9,8},{10,9},{11,10},{12... | collective-permute-start | bytes 61448 | tf_op jit(solution)/shard_map/ppermute | solution.py:22
  132.8 17.1 %collective-permute-start.16 = (bf16[8,1,8,128]{3,2,0,1:T(8,128)(2,1)S(1)}, bf16[8,1,8,128]{3,2,0,1:T(8,128)(2,1)S(1)}, u32[]{:S(2)}, u32[]{:S(2)}) collective-permute-start(bf16[8,1,8,128]{3,2,0,1:T(8,128)(2,1)S(1)} %get-tuple-element.147), channel_id=1, source_target_pairs={{0,8},{8,16},{16,24},{24,32},{32,40},{40,48},{48,56},{56,64},{64,7... | collective-permute-start | bytes 49160 | tf_op jit(solution)/shard_map/ppermute | solution.py:19
  141.2 8.7 %collective-permute-start.17 = (bf16[8,1,8,128]{3,2,0,1:T(8,128)(2,1)S(1)}, bf16[8,1,8,128]{3,2,0,1:T(8,128)(2,1)S(1)}, u32[]{:S(2)}, u32[]{:S(2)}) collective-permute-start(bf16[8,1,8,128]{3,2,0,1:T(8,128)(2,1)S(1)} %get-tuple-element.148), channel_id=1, source_target_pairs={{8,0},{16,8},{24,16},{32,24},{40,32},{48,40},{56,48},{64,56},{72,6... | collective-permute-start | bytes 49160 | tf_op jit(solution)/shard_map/ppermute | solution.py:22
  143.3 11.6 %collective-permute-start.32 = (bf16[8,1,8,128]{3,2,0,1:T(8,128)(2,1)S(1)}, bf16[8,1,8,128]{3,2,0,1:T(8,128)(2,1)S(1)}, u32[]{:S(2)}, u32[]{:S(2)}) collective-permute-start(bf16[8,1,8,128]{3,2,0,1:T(8,128)(2,1)S(1)} %get-tuple-element.155), channel_id=1, source_target_pairs={{0,8},{8,16},{16,24},{24,32},{32,40},{40,48},{48,56},{56,64},{64,7... | collective-permute-start | bytes 49160 | tf_op jit(solution)/shard_map/ppermute | solution.py:19
  150.0 11.2 %collective-permute-start.18 = (bf16[8,10,1,128]{3,2,0,1:T(2,128)(2,1)S(1)}, bf16[8,10,1,128]{3,2,0,1:T(2,128)(2,1)S(1)}, u32[]{:S(2)}, u32[]{:S(2)}) collective-permute-start(bf16[8,10,1,128]{3,2,0,1:T(2,128)(2,1)S(1)} %get-tuple-element.131), channel_id=1, source_target_pairs={{0,1},{1,2},{2,3},{3,4},{4,5},{5,6},{6,7},{8,9},{9,10},{10,11},{11... | collective-permute-start | bytes 61448 | tf_op jit(solution)/shard_map/ppermute | solution.py:19
  156.3 17.0 %collective-permute-start.34 = (bf16[8,10,1,128]{3,2,0,1:T(2,128)(2,1)S(1)}, bf16[8,10,1,128]{3,2,0,1:T(2,128)(2,1)S(1)}, u32[]{:S(2)}, u32[]{:S(2)}) collective-permute-start(bf16[8,10,1,128]{3,2,0,1:T(2,128)(2,1)S(1)} %get-tuple-element.139), channel_id=1, source_target_pairs={{0,1},{1,2},{2,3},{3,4},{4,5},{5,6},{6,7},{8,9},{9,10},{10,11},{11... | collective-permute-start | bytes 61448 | tf_op jit(solution)/shard_map/ppermute | solution.py:19
  159.9 13.4 %collective-permute-start.35 = (bf16[8,10,1,128]{3,2,0,1:T(2,128)(2,1)S(1)}, bf16[8,10,1,128]{3,2,0,1:T(2,128)(2,1)S(1)}, u32[]{:S(2)}, u32[]{:S(2)}) collective-permute-start(bf16[8,10,1,128]{3,2,0,1:T(2,128)(2,1)S(1)} %get-tuple-element.140), channel_id=1, source_target_pairs={{1,0},{2,1},{3,2},{4,3},{5,4},{6,5},{7,6},{9,8},{10,9},{11,10},{12... | collective-permute-start | bytes 61448 | tf_op jit(solution)/shard_map/ppermute | solution.py:22
  164.2 17.6 %all-to-all-start = ((bf16[32,8,8,128]{3,2,0,1:T(8,128)(2,1)}), bf16[32,8,8,128]{3,2,0,1:T(8,128)(2,1)S(1)}, u32[]{:S(2)}, u32[]{:S(2)}) async-start(bf16[32,8,8,128]{3,2,0,1:T(8,128)(2,1)} %pad_maximum_fusion.1), calls=%async_computation | async-start | bytes 1048576 | tf_op jit(solution)/shard_map/all_to_all | solution.py:162
  181.8 260.6 %all-to-all-start.1 = ((bf16[32,8,8,128]{3,2,0,1:T(8,128)(2,1)}), bf16[32,8,8,128]{3,2,0,1:T(8,128)(2,1)S(1)}, u32[]{:S(2)}, u32[]{:S(2)}) async-start(bf16[32,8,8,128]{3,2,0,1:T(8,128)(2,1)} %pad_maximum_fusion.2), calls=%async_computation.1 | async-start | bytes 1048576 | tf_op jit(solution)/shard_map/all_to_all | solution.py:162
  (31 other events, 560.8 us)
where the time goes:
time: 688 us; the launch traced here: 678 us
  blocking collectives  312 us (45%)
  other arithmetic  146 us (21%)
  starting transfers between devices  129 us (19%)
  matrix products  47.9 us (7%)
  local copies, waits for them, and re-layouts  19.7 us (3%)
  waiting for transfers between devices  17.6 us (3%)
    psum x2, blocking collectives, compress(): coeffs = lax.psum(local_proj, ('gx', 'sec')) / rows_total  163 us
    psum x2, blocking collectives, compress(): lax.psum(jnp.dot(resid, resid.T, precision=lax.Precision.HIGHEST), ('gx',...  149 us
    ppermute x18, starting transfers between devices, with_halo(): lax.ppermute(lax.slice_in_dim(block, block.shape[dim] - width, None, axis...  87.7 us
    another operation x14, other arithmetic, small_rotation(): factor = jnp.linalg.cholesky(inner)  69.6 us
    another operation x5, other arithmetic, small_rotation(): lax.linalg.triangular_solve(factor, leading.T, left_side=True, lower=True)  40 us
    ppermute x18, starting transfers between devices, with_halo(): lax.ppermute(lax.slice_in_dim(block, 0, width, axis=dim), axis, backward)  29.1 us
  transfers between devices with their start and end apart: 38, of which 8 were waited for; matrix products, arithmetic and copies ran while one was open for 18% of the time, Pallas kernels for 0%

commit v1 on v0

--- a/solution.py
+++ b/solution.py
@@ -77,7 +77,10 @@
         rounded, flat_basis, (((1,), (1,)), ((), ())), preferred_element_type=jnp.float32
     )
     gram = (
-        lax.psum(jnp.dot(resid, resid.T, precision=lax.Precision.HIGHEST), ("gx", "sec"))
+        jnp.sum(
+            lax.all_gather(jnp.dot(resid, resid.T, precision=lax.Precision.HIGHEST), ("gx", "sec")),
+            axis=0,
+        )
         / rows_total
     )
     lower = jnp.linalg.cholesky(gram)

time: 688 us -> 1960 us (2.85)
  waiting for transfers between devices: 17.6 us -> 1430 us
  blocking collectives: 312 us -> 164 us
    all_gather x0 -> x2, waiting for transfers between devices: none -> 1400 us  [compress(): lax.all_gather(jnp.dot(resid, resid.T, precision=lax.Precision.HIGHEST),...]
    psum x2 -> x0, blocking collectives: 149 us -> none  [compress(): lax.psum(jnp.dot(resid, resid.T, precision=lax.Precision.HIGHEST), ('gx',...]
  transfers between devices with their start and end apart: 38 -> 40, of which waited for: 8 -> 10; matrix products, arithmetic and copies ran while one was open for 18% -> 2% of each run, Pallas kernels for 0% -> 0%
where the time goes in v1:
time: 1960 us; the launch traced here: 1950 us
  waiting for transfers between devices  1430 us (73%)
  blocking collectives  164 us (8%)
  other arithmetic  146 us (7%)
  starting transfers between devices  135 us (7%)
  matrix products  37.5 us (2%)
  local copies, waits for them, and re-layouts  23.4 us (1%)
    all_gather x2, waiting for transfers between devices, compress(): lax.all_gather(jnp.dot(resid, resid.T, precision=lax.Precision.HIGHEST),...  1400 us
    psum x2, blocking collectives, compress(): coeffs = lax.psum(local_proj, ('gx', 'sec')) / rows_total  164 us
    ppermute x18, starting transfers between devices, with_halo(): lax.ppermute(lax.slice_in_dim(block, block.shape[dim] - width, None, axis...  89.5 us
    another operation x14, other arithmetic, small_rotation(): factor = jnp.linalg.cholesky(inner)  69.6 us
    another operation x5, other arithmetic, small_rotation(): lax.linalg.triangular_solve(factor, leading.T, left_side=True, lower=True)  39.4 us
  transfers between devices with their start and end apart: 40, of which 10 were waited for; matrix products, arithmetic and copies ran while one was open for 2% of the time, Pallas kernels for 0%

profile of v1, /device:TPU:1, one launch (start us, length us, event | category | flops | bytes accessed | tf_op | source)
XLA Modules:
  0.0 1950.4 jit_solution(16484564361644021407)
XLA Ops:
  8.6 6.3 collective-permute-start
  17.9 4.5 collective-permute-start.4
  60.7 6.4 collective-permute-start.8
  69.1 4.5 collective-permute-start.24
  80.9 5.1 collective-permute-start.26
  96.2 7.8 collective-permute-start.12
  126.0 7.5 collective-permute-start.16
  140.2 6.4 collective-permute-start.18
  154.2 9.7 all-to-all-start
  166.2 7.6 collective-permute-start.32
  180.7 84.3 %psum.14 = f32[32,256]{1,0:T(8,128)S(1)} all-reduce(f32[32,256]{1,0:T(8,128)S(1)} %fusion.9), channel_id=1, replica_groups=mesh['gx'=32,'sec'=8] {'gx','sec'}, use_global_device_ids=true, to_apply=%region_0.1 | all-reduce | flops 8192 | bytes 65536 | tf_op jit(solution)/shard_map/psum | solution.py:74
  281.2 6.5 all-to-all-start.1
  288.3 6.4 all-to-all-done.1
  294.9 687.8 %all-gather.5.cloned.1.call-done = f32[8192,32]{1,0:T(8,128)} async-done(((f32[32,32]{1,0:T(8,128)}), f32[8192,32]{1,0:T(8,128)}) %all-gather.5.cloned.1.call-update) | async-done | bytes 1048592 | tf_op jit(solution)/shard_map/all_gather | solution.py:81
  994.9 11.7 cholesky.183
  1007.3 9.8 custom-call.19
  1017.6 11.9 cholesky.200
  1035.6 19.7 %custom-call.20 = f32[2,128,128]{1,2,0:T(8,128)S(1)} custom-call(f32[2,128,128]{2,1,0:T(8,128)S(1)} %get-tuple-element.21), custom_call_target="InvertDiagBlocksLowerTriangular" | custom-call | tf_op jit(solution)/shard_map/triangular_solve/custom-call.4 | solution.py:63
  1064.4 79.3 %psum.15 = f32[32,256]{1,0:T(8,128)S(1)} all-reduce(f32[32,256]{1,0:T(8,128)S(1)} %fusion.7), channel_id=1, replica_groups=mesh['gx'=32,'sec'=8] {'gx','sec'}, use_global_device_ids=true, to_apply=%region_9.14 | all-reduce | flops 8192 | bytes 65536 | tf_op jit(solution)/shard_map/psum | solution.py:74
  1150.4 711.0 %all-gather.7.cloned.1.call-done = f32[8192,32]{1,0:T(8,128)} async-done(((f32[32,32]{1,0:T(8,128)}), f32[8192,32]{1,0:T(8,128)}) %all-gather.7.cloned.1.call-update) | async-done | bytes 1048592 | tf_op jit(solution)/shard_map/all_gather | solution.py:81
  1870.1 11.7 cholesky.228
  1882.5 9.8 custom-call.22
  1892.8 12.0 cholesky.245
  1910.8 19.7 %custom-call.23 = f32[2,128,128]{1,2,0:T(8,128)S(1)} custom-call(f32[2,128,128]{2,1,0:T(8,128)S(1)} %get-tuple-element.22), custom_call_target="InvertDiagBlocksLowerTriangular" | custom-call | tf_op jit(solution)/shard_map/triangular_solve/custom-call.4 | solution.py:63
  (292 shorter events, 192.5 us)
Async XLA Ops:
  8.6 26.9 %collective-permute-start = (bf16[1,8,128]{2,1,0:T(8,128)(2,1)S(1)}, bf16[1,8,128]{2,1,0:T(8,128)(2,1)S(1)}, u32[]{:S(2)}, u32[]{:S(2)}) collective-permute-start(bf16[1,8,128]{2,1,0:T(8,128)(2,1)S(1)} %get-tuple-element.179), channel_id=1, source_target_pairs={{0,8},{8,16},{16,24},{24,32},{32,40},{40,48},{48,56},{56,64},{64,7... | collective-permute-start | bytes 6152 | tf_op jit(solution)/shard_map/ppermute | solution.py:19
  14.8 20.6 %collective-permute-start.1 = (bf16[1,8,128]{2,1,0:T(8,128)(2,1)S(1)}, bf16[1,8,128]{2,1,0:T(8,128)(2,1)S(1)}, u32[]{:S(2)}, u32[]{:S(2)}) collective-permute-start(bf16[1,8,128]{2,1,0:T(8,128)(2,1)S(1)} %get-tuple-element.180), channel_id=1, source_target_pairs={{8,0},{16,8},{24,16},{32,24},{40,32},{48,40},{56,48},{64,56},{72,6... | collective-permute-start | bytes 6152 | tf_op jit(solution)/shard_map/ppermute | solution.py:22
  17.9 25.7 %collective-permute-start.4 = (bf16[8,1,8,128]{3,2,0,1:T(8,128)(2,1)S(1)}, bf16[8,1,8,128]{3,2,0,1:T(8,128)(2,1)S(1)}, u32[]{:S(2)}, u32[]{:S(2)}) collective-permute-start(bf16[8,1,8,128]{3,2,0,1:T(8,128)(2,1)S(1)} %get-tuple-element.153), channel_id=1, source_target_pairs={{0,8},{8,16},{16,24},{24,32},{32,40},{40,48},{48,56},{56,64},{64,7... | collective-permute-start | bytes 49160 | tf_op jit(solution)/shard_map/ppermute | solution.py:19
  22.4 21.1 %collective-permute-start.5 = (bf16[8,1,8,128]{3,2,0,1:T(8,128)(2,1)S(1)}, bf16[8,1,8,128]{3,2,0,1:T(8,128)(2,1)S(1)}, u32[]{:S(2)}, u32[]{:S(2)}) collective-permute-start(bf16[8,1,8,128]{3,2,0,1:T(8,128)(2,1)S(1)} %get-tuple-element.154), channel_id=1, source_target_pairs={{8,0},{16,8},{24,16},{32,24},{40,32},{48,40},{56,48},{64,56},{72,6... | collective-permute-start | bytes 49160 | tf_op jit(solution)/shard_map/ppermute | solution.py:22
  24.4 23.8 %collective-permute-start.20 = (bf16[8,1,8,128]{3,2,0,1:T(8,128)(2,1)S(1)}, bf16[8,1,8,128]{3,2,0,1:T(8,128)(2,1)S(1)}, u32[]{:S(2)}, u32[]{:S(2)}) collective-permute-start(bf16[8,1,8,128]{3,2,0,1:T(8,128)(2,1)S(1)} %get-tuple-element.161), channel_id=1, source_target_pairs={{0,8},{8,16},{16,24},{24,32},{32,40},{40,48},{48,56},{56,64},{64,7... | collective-permute-start | bytes 49160 | tf_op jit(solution)/shard_map/ppermute | solution.py:19
  43.6 9.9 collective-permute-start.6
  60.7 15.0 collective-permute-start.8
  67.0 8.7 collective-permute-start.9
  69.1 11.6 collective-permute-start.24
  75.8 11.5 collective-permute-start.10
  96.2 16.5 collective-permute-start.12
  104.0 8.7 collective-permute-start.13
  106.1 11.6 collective-permute-start.28
  110.6 8.4 collective-permute-start.29
  112.8 11.6 collective-permute-start.14
  119.1 16.4 collective-permute-start.30
  122.9 12.6 collective-permute-start.31
  126.0 9.7 collective-permute-start.16
  154.2 22.3 %all-to-all-start = ((bf16[32,8,8,128]{3,2,0,1:T(8,128)(2,1)}), bf16[32,8,8,128]{3,2,0,1:T(8,128)(2,1)}, u32[]{:S(2)}, u32[]{:S(2)}) async-start(bf16[32,8,8,128]{3,2,0,1:T(8,128)(2,1)} %pad_maximum_fusion.1), calls=%async_computation | async-start | bytes 1048576 | tf_op jit(solution)/shard_map/all_to_all | solution.py:165
  163.9 818.8 %all-gather.5.cloned.1.call-start = ((), (), s32[]{:S(2)}) async-start(), calls=%async_computation.2 | async-start | bytes 4210688 | tf_op jit(solution)/shard_map/all_gather | solution.py:81
  166.2 104.1 %collective-permute-start.32 = (bf16[8,1,8,128]{3,2,0,1:T(8,128)(2,1)S(1)}, bf16[8,1,8,128]{3,2,0,1:T(8,128)(2,1)S(1)}, u32[]{:S(2)}, u32[]{:S(2)}) collective-permute-start(bf16[8,1,8,128]{3,2,0,1:T(8,128)(2,1)S(1)} %get-tuple-element.155), channel_id=1, source_target_pairs={{0,8},{8,16},{16,24},{24,32},{32,40},{40,48},{48,56},{56,64},{64,7... | collective-permute-start | bytes 49160 | tf_op jit(solution)/shard_map/ppermute | solution.py:19
  173.8 96.5 %collective-permute-start.33 = (bf16[8,1,8,128]{3,2,0,1:T(8,128)(2,1)S(1)}, bf16[8,1,8,128]{3,2,0,1:T(8,128)(2,1)S(1)}, u32[]{:S(2)}, u32[]{:S(2)}) collective-permute-start(bf16[8,1,8,128]{3,2,0,1:T(8,128)(2,1)S(1)} %get-tuple-element.156), channel_id=1, source_target_pairs={{8,0},{16,8},{24,16},{32,24},{40,32},{48,40},{56,48},{64,56},{72,6... | collective-permute-start | bytes 49160 | tf_op jit(solution)/shard_map/ppermute | solution.py:22
  281.2 13.6 all-to-all-start.1
  287.6 1573.8 %all-gather.7.cloned.1.call-start = ((), (), s32[]{:S(2)}) async-start(), calls=%async_computation.3 | async-start | bytes 4210688 | tf_op jit(solution)/shard_map/all_gather | solution.py:81
  (34 other events, 1763.6 us)
Sparse Core Ops, SparseCore 0:
  270.2 712.3 all-gather.4
  1148.5 712.8 all-gather.6
